TPU v7x, 32 devices: a whole 2x2x4 slice. The times are simulated.
32 devices in a mesh: shot: 4 (over y, core), depth: 8 (over z, x).
Axes of the slice: x: 2, y: 2, z: 4, core: 2. Of those that a mesh axis runs over, the one named last changes fastest.
Arguments:
- grad_part: float32 [4, 256, 8192], P('shot', 'depth'), may hold values from -6 to 6
- illum_part: float32 [4, 256, 8192], P('shot', 'depth'), may hold values from 0.1 to 1
- source_count: int32 [4], P('shot'), may hold values from 1 to 8
- rate: float32 [8192], P('shot'), may hold values from 0.00078125 to 0.03
- coef_table: float32 [64], replicated, may hold values from 0.2 to 1
- coef_index: int32 [256], P('depth'), may hold values from 0 to 63
Outputs:
- image: float32 [256, 8192], P('depth', 'shot')
All inputs are finite; a program needn't handle non-finite values.
Results may differ from a plain program's by a relative error of at most 0.0003.
Values sent between devices are 32-bit elements; how exact they have to be, the bound alone decides.
A program may use at most 64 MiB of HBM per device.

v0:
```python
import jax
import jax.numpy as jnp
from jax import lax
from jax.sharding import PartitionSpec as P


def entering_2(x, axis, combine, identity, reverse):
    count, index = (lax.axis_size(axis), lax.axis_index(axis))
    everything = jax.tree.map(lambda part: lax.all_gather(part, axis), x)
    start = jax.tree.map(
        lambda part, zero: jnp.broadcast_to(jnp.asarray(zero, part.dtype), part.shape), x, identity
    )

    def step(k, before):
        at = count - 1 - k if reverse else k
        reached = at > index if reverse else at < index
        new = combine(before, jax.tree.map(lambda part: part[at], everything))
        return jax.tree.map(lambda a, b: jnp.where(reached, a, b), new, before)

    return lax.fori_loop(0, count, step, start)


def combine(earlier, later):
    return (earlier[0] * later[0], later[0] * earlier[1] + later[1])


def shards(grad_part, illum_part, source_count, rate, coef_table, coef_index):
    weight = 1.0 / source_count.astype(jnp.float32)
    scaled = grad_part[0] * weight[0]
    summed, lights = (
        lax.psum_scatter(scaled, "shot", scatter_dimension=1, tiled=True),
        lax.psum_scatter(illum_part[0], "shot", scatter_dimension=1, tiled=True),
    )
    quotient = summed / lights
    levels = jnp.arange(coef_table.shape[0], dtype=jnp.int32)
    picked = jnp.sum(
        jnp.where(coef_index[:, None] == levels[None, :], coef_table[None, :], 0.0), axis=1
    )
    factor = jnp.exp(-(picked[:, None] * rate[None, :]))
    ones = jnp.ones((factor.shape[1],), jnp.float32)
    zeros = jnp.zeros((factor.shape[1],), jnp.float32)
    product, local_down = lax.associative_scan(combine, (factor, (1.0 - factor) * quotient), axis=0)
    _, entering = entering_2((product[-1], local_down[-1]), "depth", combine, (ones, zeros), False)
    smooth = local_down + product * entering[None, :]
    upward, local_up = lax.associative_scan(
        combine, (factor, (1.0 - factor) * smooth), reverse=True, axis=0
    )
    _, arriving = entering_2((upward[0], local_up[0]), "depth", combine, (ones, zeros), True)
    return local_up + upward * arriving[None, :]


def solution(mesh):
    placed = (
        P("shot", "depth", None),
        P("shot", "depth", None),
        P("shot"),
        P("shot"),
        P(),
        P("depth"),
    )
    return jax.shard_map(
        shards, mesh=mesh, in_specs=placed, out_specs=P("depth", "shot"), check_vma=False
    )
```

profile of v0, /device:TPU:0, one launch (start us, length us, event | category | flops | bytes accessed | tf_op | source)
XLA Modules:
  0.0 204.0 jit_solution(4261898000439314385)
XLA Ops:
  7.2 2.3 %multiply_bitcast_fusion = f32[32,8192]{1,0:T(8,128)} fusion(f32[1,32,8192]{2,1,0:T(8,128)} %param.10, f32[]{:T(128)} %bitcast), kind=kLoop, calls=%fused_computation.6 | loop fusion | flops 262144 | bytes 2097156 | tf_op jit(solution)/shard_map/mul | solution.py:29
  9.5 0.0 reduce-scatter.3.cloned.1.call-update
  9.6 0.0 reduce-scatter.5.cloned.1.call-start
  9.6 0.7 reduce-scatter.5.cloned.1.call-update
  10.4 0.6 copy-done.1
  11.0 0.0 copy-done.2
  11.0 0.2 select_reduce_fusion
  11.2 26.2 %reduce-scatter.3.cloned.1.call-done = f32[32,2048]{1,0:T(8,128)} async-done(((f32[32,8192]{1,0:T(8,128)}), f32[32,2048]{1,0:T(8,128)}) %reduce-scatter.3.cloned.1.call-update) | async-done | bytes 262160 | tf_op jit(solution)/shard_map/reduce_scatter | solution.py:31
  37.4 27.3 %reduce-scatter.5.cloned.1.call-done = f32[32,2048]{1,0:T(8,128)} async-done(((f32[32,8192]{1,0:T(8,128)}), f32[32,2048]{1,0:T(8,128)}) %reduce-scatter.5.cloned.1.call-update) | async-done | bytes 262160 | tf_op jit(solution)/shard_map/reduce_scatter | solution.py:32
  64.7 1.1 divide_multiply_fusion
  66.6 0.1 fusion.19
  66.9 0.1 slice.311
  67.0 0.1 slice.344
  68.0 30.6 %all-gather.1 = f32[8,1,2048]{2,1,0:T(1,128)S(1)} all-gather(f32[1,1,2048]{2,1,0:T(1,128)S(1)} %add_bitcast_fusion.2), channel_id=1, replica_groups=mesh['shot'=4,'depth'=8] {'depth'}, dimensions={0}, use_global_device_ids=true | all-gather | bytes 73728 | tf_op jit(solution)/shard_map/all_gather | solution.py:9
  98.8 30.5 %all-gather = f32[8,1,2048]{2,1,0:T(1,128)S(1)} all-gather(f32[1,1,2048]{2,1,0:T(1,128)S(1)} %add_bitcast_fusion.3), channel_id=1, replica_groups=mesh['shot'=4,'depth'=8] {'depth'}, dimensions={0}, use_global_device_ids=true | all-gather | bytes 73728 | tf_op jit(solution)/shard_map/all_gather | solution.py:9
  129.3 0.5 while.30
  129.8 0.1 add_multiply_fusion
  130.1 0.3 slice.359
  130.3 0.3 slice.365
  130.6 0.3 slice.361
  130.9 0.3 slice.363
  131.8 0.1 fusion.17
  132.0 0.1 slice.393
  132.1 0.1 slice.357
  132.9 0.4 slice.394
  133.3 0.4 slice.358
  134.1 30.5 %all-gather.3 = f32[8,1,2048]{2,1,0:T(1,128)S(1)} all-gather(f32[1,1,2048]{2,1,0:T(1,128)S(1)} %add_bitcast_fusion), channel_id=1, replica_groups=mesh['shot'=4,'depth'=8] {'depth'}, dimensions={0}, use_global_device_ids=true | all-gather | bytes 73728 | tf_op jit(solution)/shard_map/all_gather | solution.py:9
  164.7 30.5 %all-gather.2 = f32[8,1,2048]{2,1,0:T(1,128)S(1)} all-gather(f32[1,1,2048]{2,1,0:T(1,128)S(1)} %add_bitcast_fusion.1), channel_id=1, replica_groups=mesh['shot'=4,'depth'=8] {'depth'}, dimensions={0}, use_global_device_ids=true | all-gather | bytes 73728 | tf_op jit(solution)/shard_map/all_gather | solution.py:9
  195.3 0.6 while.31
  195.8 0.3 rev.9
  196.1 0.3 rev.8
  196.4 0.7 multiply_add_fusion
  (176 shorter events, 3.8 us)
Async XLA Ops:
  6.5 30.9 %reduce-scatter.3.cloned.1.call-start = ((), (), s32[]{:S(2)}) async-start(), calls=%async_computation.2 | async-start | bytes 1310720 | tf_op jit(solution)/shard_map/reduce_scatter | solution.py:31
  9.6 55.2 %reduce-scatter.5.cloned.1.call-start = ((), (), s32[]{:S(2)}) async-start(), calls=%async_computation.3 | async-start | bytes 1310720 | tf_op jit(solution)/shard_map/reduce_scatter | solution.py:32
  10.3 54.4 %copy-start = (f32[2048]{0:T(1024)S(1)}, f32[2048]{0:T(1024)}, u32[]{:S(2)}) copy-start(f32[2048]{0:T(1024)} %param.13) | copy-start | bytes 24580
  10.4 0.7 copy-start.1
  10.4 0.7 copy-start.2
Sparse Core Ops, SparseCore 0:
  9.9 27.4 reduce-scatter.2
  39.9 24.7 reduce-scatter.4
where the time goes:
time: 204 us
  blocking collectives  122 us (60%)
  waiting for transfers between devices  54.2 us (27%)
  between operations  15.1 us (7%)
  local copies, waits for them, and re-layouts  5.94 us (3%)
  other arithmetic  5.84 us (3%)
    all_gather x4, blocking collectives, entering_2(): everything = jax.tree.map(lambda part: lax.all_gather(part, axis), x)  122 us
    reduce_scatter x1, waiting for transfers between devices, shards(): lax.psum_scatter(illum_part[0], 'shot', scatter_dimension=1, tiled=True)  27.3 us
    reduce_scatter x1, waiting for transfers between devices, shards(): lax.psum_scatter(scaled, 'shot', scatter_dimension=1, tiled=True)  26.2 us
  transfers between devices with their start and end apart: 2, of which 2 were waited for; matrix products, arithmetic and copies ran while one was open for 0% of the time, Pallas kernels for 0%

commit v1 on v0

v1 whole, which is shorter than its diff:
```python
import functools

import jax
import jax.numpy as jnp
from jax import lax
from jax.experimental import pallas as pl
from jax.experimental.pallas import tpu as pltpu
from jax.sharding import PartitionSpec as P

MESH = pl.DeviceIdType.MESH
LANES = 128
SUB = 8


def body(
    dims,
    grad, illum, count, rate, table, index, out,
    own, part, sums, landed, early, late, inject, weigh, back, reach, held, states, weights,
    own_sem, part_send, part_recv, sums_send, sums_recv,
    early_send, early_recv, late_send, late_recv, w_send, w_recv,
):
    ys, ks, rows, width, chunks = dims
    cw = width // chunks
    cols = cw // LANES
    tiles = rows // SUB
    me = lax.axis_index("shot")
    d = lax.axis_index("depth")
    y, c = me // 2, me % 2
    mate = y * 2 + 1 - c

    def peer(i):
        return lax.rem(d + i, ks)

    def other(i):
        return lax.rem(y + i, ys)

    barrier = pltpu.get_barrier_semaphore()
    pl.semaphore_signal(barrier, inc=1, device_id=(mate, d), device_id_type=MESH)
    for i in range(1, ys):
        pl.semaphore_signal(barrier, inc=1, device_id=(other(i) * 2 + c, d), device_id_type=MESH)
    for i in range(1, ks):
        pl.semaphore_signal(barrier, inc=1, device_id=(me, peer(i)), device_id_type=MESH)

    def slab(src, target, core, ch):
        at = pl.multiple_of((target * 2 + core) * width + ch * cw, LANES)
        return src.at[0, :, pl.ds(at, cw)]

    order = [(i, ch) for i in [*range(1, ys), 0] for ch in range(chunks)]

    def own_copy(i, ch, a):
        return pltpu.make_async_copy(
            slab((grad, illum)[a], other(i), c, ch), own.at[i, ch, a], own_sem.at[i, ch, a]
        )

    def part_copy(i, ch, a):
        return pltpu.make_async_remote_copy(
            src_ref=slab((grad, illum)[a], other(i), 1 - c, ch),
            dst_ref=part.at[i, ch, a],
            send_sem=part_send.at[i, ch, a],
            recv_sem=part_recv.at[i, ch, a],
            device_id=(mate, d),
            device_id_type=MESH,
        )

    def sums_copy(i, ch):
        return pltpu.make_async_remote_copy(
            src_ref=sums.at[i - 1, ch],
            dst_ref=landed.at[i - 1, ch],
            send_sem=sums_send.at[i - 1, ch],
            recv_sem=sums_recv.at[i - 1, ch],
            device_id=(other(i) * 2 + c, d),
            device_id_type=MESH,
        )

    def early_copy(i):
        return pltpu.make_async_remote_copy(
            src_ref=early.at[0],
            dst_ref=early.at[ks - i],
            send_sem=early_send.at[i - 1],
            recv_sem=early_recv.at[ks - i - 1],
            device_id=(me, peer(i)),
            device_id_type=MESH,
        )

    def late_copy(i, ch):
        return pltpu.make_async_remote_copy(
            src_ref=late.at[0, ch],
            dst_ref=late.at[ks - i, ch],
            send_sem=late_send.at[i - 1, ch],
            recv_sem=late_recv.at[ks - i - 1, ch],
            device_id=(me, peer(i)),
            device_id_type=MESH,
        )

    w_copy = pltpu.make_async_remote_copy(
        src_ref=weights.at[0],
        dst_ref=weights.at[1],
        send_sem=w_send,
        recv_sem=w_recv,
        device_id=(mate, d),
        device_id_type=MESH,
    )

    for i, ch in order:
        for a in range(2):
            own_copy(i, ch, a).start()
    weights[0] = 1.0 / jnp.full((SUB, LANES), count[0], jnp.int32).astype(jnp.float32)

    pl.semaphore_wait(barrier, ys + ks - 1)
    w_copy.start()
    for i, ch in order:
        for a in range(2):
            part_copy(i, ch, a).start()

    sub = lax.broadcasted_iota(jnp.int32, (SUB, LANES), 0)

    def prefix(v):
        for s in (1, 2, 4):
            v = v + jnp.where(sub >= s, pltpu.roll(v, s, 0), 0.0)
        return v

    def suffix(v):
        for s in (1, 2, 4):
            v = v + jnp.where(sub < SUB - s, pltpu.roll(v, SUB - s, 0), 0.0)
        return v

    def first(v):
        return jnp.broadcast_to(v[0:1], (SUB, LANES))

    def last(v):
        return jnp.broadcast_to(v[SUB - 1 : SUB], (SUB, LANES))

    coef, through, before = [], [], []
    total = jnp.zeros((SUB, LANES), jnp.float32)
    for t in range(tiles):
        v = jnp.zeros((SUB, LANES), jnp.float32)
        for r in range(SUB):
            v = jnp.where(sub == r, table[index[t * SUB + r]], v)
        run = prefix(v) + total
        coef.append(v)
        through.append(run)
        before.append(run - v)
        total = last(run)

    def terms():
        for j in range(width // LANES):
            at = pl.ds(j * LANES, LANES)
            ch, jj = j // cols, j % cols
            r = jnp.broadcast_to(rate[0:1, at], (SUB, LANES))
            tail = jnp.zeros((SUB, LANES), jnp.float32)
            for t in reversed(range(tiles)):
                zs = pl.ds(t * SUB, SUB)
                rest = 1.0 - jnp.exp(-(coef[t] * r))
                inject[zs, at] = rest * jnp.exp(through[t] * r)
                h = rest * jnp.exp(-((through[t] + before[t]) * r))
                weigh[zs, at] = h
                lift = jnp.exp(before[t] * r)
                back[zs, at] = lift
                run = suffix(h) + tail
                reach[zs, at] = lift * run
                tail = first(run)
            early[0, 0, pl.ds(j, 1), :] = jnp.exp(-(total * r))[0:1]
            early[0, 1, pl.ds(j, 1), :] = tail[0:1]

    def reduced(i, ch, a, zs, at):
        if a == 0:
            w, v = weights[0], weights[1]
            return own[i, ch, 0, zs, at] * w + part[i, ch, 0, zs, at] * v
        return own[i, ch, 1, zs, at] + part[i, ch, 1, zs, at]

    def arrived(i, ch):
        for a in range(2):
            own_copy(i, ch, a).wait()
            part_copy(i, ch, a).wait_recv()

    w_copy.wait_recv()
    for n, (i, ch) in enumerate(order[: (ys - 1) * chunks]):
        arrived(i, ch)
        for j in range(cols):
            at = pl.ds(j * LANES, LANES)
            for t in range(tiles):
                zs = pl.ds(t * SUB, SUB)
                for a in range(2):
                    sums[i - 1, ch, a, zs, at] = reduced(i, ch, a, zs, at)
        sums_copy(i, ch).start()

    terms()
    for i in range(1, ks):
        early_copy(i).start()

    for ch in range(chunks):
        arrived(0, ch)
        for i in range(1, ys):
            sums_copy(i, ch).wait_recv()
        for j in range(cols):
            at = pl.ds(j * LANES, LANES)
            full = pl.ds(ch * cw + j * LANES, LANES)
            carry = jnp.zeros((SUB, LANES), jnp.float32)
            parts = []
            for t in range(tiles):
                zs = pl.ds(t * SUB, SUB)
                num, den = reduced(0, ch, 0, zs, at), reduced(0, ch, 1, zs, at)
                for i in range(1, ys):
                    num = num + landed[i - 1, ch, 0, zs, at]
                    den = den + landed[i - 1, ch, 1, zs, at]
                run = prefix(inject[zs, full] * (num / den)) + carry
                parts.append(run)
                carry = last(run)
            row = pl.ds(ch * cols + j, 1)
            late[0, ch, 0, pl.ds(j, 1), :] = carry[0:1] * early[0, 0, row, :]
            tail = jnp.zeros((SUB, LANES), jnp.float32)
            for t in reversed(range(tiles)):
                zs = pl.ds(t * SUB, SUB)
                run = suffix(weigh[zs, full] * parts[t]) + tail
                held[zs, full] = run
                tail = first(run)
            late[0, ch, 1, pl.ds(j, 1), :] = tail[0:1]
        for i in range(1, ks):
            late_copy(i, ch).start()

    for i in range(1, ks):
        early_copy(i).wait_recv()

    for ch in range(chunks):
        for i in range(1, ks):
            late_copy(i, ch).wait_recv()
        rs = pl.ds(ch * cols, cols)
        state = jnp.zeros((cols, LANES), jnp.float32)
        mine = state
        ups = []
        for k in range(ks):
            slot = lax.rem(k - d + ks, ks)
            mine = jnp.where(k == d, state, mine)
            ups.append(late[slot, ch, 1] + early[slot, 1, rs] * state)
            if k < ks - 1:
                state = late[slot, ch, 0] + early[slot, 0, rs] * state
        up = jnp.zeros((cols, LANES), jnp.float32)
        for k in reversed(range(1, ks)):
            slot = lax.rem(k - d + ks, ks)
            up = jnp.where(k > d, ups[k] + early[slot, 0, rs] * up, up)
        states[0, rs] = mine
        states[1, rs] = up * early[0, 0, rs]
        for j in range(cols):
            row = pl.ds(ch * cols + j, 1)
            full = pl.ds(ch * cw + j * LANES, LANES)
            e = jnp.broadcast_to(states[0, row, :], (SUB, LANES))
            b = jnp.broadcast_to(states[1, row, :], (SUB, LANES))
            for t in range(tiles):
                zs = pl.ds(t * SUB, SUB)
                out[zs, full] = back[zs, full] * (held[zs, full] + b) + reach[zs, full] * e

    w_copy.wait_send()
    for i, ch in order:
        for a in range(2):
            part_copy(i, ch, a).wait_send()
        if i:
            sums_copy(i, ch).wait_send()
    for i in range(1, ks):
        early_copy(i).wait_send()
        for ch in range(chunks):
            late_copy(i, ch).wait_send()


def shards(ys, ks, grad_part, illum_part, source_count, rate, coef_table, coef_index):
    _, rows, lateral = grad_part.shape
    width = lateral // (2 * ys)
    chunks = min(4, width // LANES)
    cw = width // chunks
    cols = cw // LANES
    f32 = jnp.float32
    dma = pltpu.SemaphoreType.DMA
    blocks = (ys, chunks, 2, rows, cw)
    peers = (ys - 1, chunks, 2, rows, cw)
    field = pltpu.VMEM((rows, width), f32)
    anywhere = pl.BlockSpec(memory_space=pl.ANY)
    scalars = pl.BlockSpec(memory_space=pltpu.SMEM)
    vmem = pl.BlockSpec(memory_space=pltpu.VMEM)
    return pl.pallas_call(
        functools.partial(body, (ys, ks, rows, width, chunks)),
        out_shape=jax.ShapeDtypeStruct((rows, width), f32),
        in_specs=[anywhere, anywhere, scalars, vmem, scalars, scalars],
        out_specs=vmem,
        scratch_shapes=[
            pltpu.VMEM(blocks, f32),
            pltpu.VMEM(blocks, f32),
            pltpu.VMEM(peers, f32),
            pltpu.VMEM(peers, f32),
            pltpu.VMEM((ks, 2, width // LANES, LANES), f32),
            pltpu.VMEM((ks, chunks, 2, cols, LANES), f32),
            field, field, field, field, field,
            pltpu.VMEM((2, width // LANES, LANES), f32),
            pltpu.VMEM((2, SUB, LANES), f32),
            dma((ys, chunks, 2)),
            dma((ys, chunks, 2)),
            dma((ys, chunks, 2)),
            dma((ys - 1, chunks)),
            dma((ys - 1, chunks)),
            dma((ks - 1,)),
            dma((ks - 1,)),
            dma((ks - 1, chunks)),
            dma((ks - 1, chunks)),
            dma,
            dma,
        ],
        compiler_params=pltpu.CompilerParams(collective_id=0, has_side_effects=True),
    )(grad_part, illum_part, source_count, rate.reshape(1, -1), coef_table, coef_index)


def solution(mesh):
    placed = (
        P("shot", "depth", None),
        P("shot", "depth", None),
        P("shot"),
        P("shot"),
        P(),
        P("depth"),
    )
    return jax.shard_map(
        functools.partial(shards, mesh.shape["shot"] // 2, mesh.shape["depth"]),
        mesh=mesh, in_specs=placed, out_specs=P("depth", "shot"), check_vma=False,
    )
```

time: 204 us -> 28.8 us (0.14)
  blocking collectives: 122 us -> 0 us
  waiting for transfers between devices: 54.2 us -> 0 us
  Pallas kernels: 0 us -> 26.2 us
  between operations: 15.1 us -> 0.66 us
  other arithmetic: 5.84 us -> 0 us
  local copies, waits for them, and re-layouts: 5.94 us -> 1.67 us
    all_gather x4 -> x0, blocking collectives: 122 us -> none  [entering_2(): everything = jax.tree.map(lambda part: lax.all_gather(part, axis), x)]
    reduce_scatter x2 -> x0, waiting for transfers between devices: 53.5 us -> none  [the longest x1 27.3 us: shards(): lax.psum_scatter(illum_part[0], 'shot', scatter_dimension=1, tiled=True)]
    pallas_call x0 -> x1, Pallas kernels: none -> 26.2 us  [shards(): pl.pallas_call(functools.partial(body, (ys, ks, rows, width, chunks)), ou...]
    mul x11 -> x0, other arithmetic: 3.81 us -> none  [the longest x1 2.31 us: shards(): scaled = grad_part[0] * weight[0]]
    slice x59 -> x0, local copies, waits for them, and re-layouts: 3.44 us -> none  [the longest x32 2.63 us: shards(): lax.associative_scan(combine, (factor, (1.0 - factor) * smooth), reverse=...]
  transfers between devices with their start and end apart: 2 -> 0, of which waited for: 2 -> 0; matrix products, arithmetic and copies ran while one was open for 0% -> 0% of each run, Pallas kernels for 0% -> 0%
where the time goes in v1:
time: 28.8 us; the launch traced here: 28.6 us
  Pallas kernels  26.2 us (91%)
  local copies, waits for them, and re-layouts  1.67 us (6%)
  between operations  0.66 us (2%)
    pallas_call x1, Pallas kernels, shards(): pl.pallas_call(functools.partial(body, (ys, ks, rows, width, chunks)), ou...  26.2 us
    unnamed x1, local copies, waits for them, and re-layouts  1.67 us

profile of v1, /device:TPU:0, one launch (start us, length us, event | category | flops | bytes accessed | tf_op | source)
XLA Modules:
  0.0 28.6 jit_solution(17879835271929250670)
XLA Ops:
  0.7 26.2 %shard_map.64 = f32[32,2048]{1,0:T(8,128)} custom-call(f32[1,32,8192]{2,1,0:T(8,128)} %grad.1, f32[1,32,8192]{2,1,0:T(8,128)} %illum.1, s32[1]{0:T(128)S(6)} %copy.8.count, f32[1,2048]{1,0:T(1,128)} %bitcast.1, f32[64]{0:T(128)} %table.1, s32[32]{0:T(128)} %index.1), custom_call_target="tpu_custom_call" | custom-call | tf_op jit(solution)/shard_map/pallas_call | solution.py:278
  26.9 1.7 %copy.9 = f32[32,2048]{1,0:T(8,128)} copy(f32[32,2048]{1,0:T(8,128)} %shard_map.64) | data formatting | bytes 524288

commit v2 on v1

--- a/solution.py
+++ b/solution.py
@@ -14,10 +14,10 @@
 
 def body(
     dims,
-    grad, illum, count, rate, table, index, out,
-    own, part, sums, landed, early, late, inject, weigh, back, reach, held, states, weights,
+    grad, illum, weight, rate, table, index, out,
+    own, part, sums, landed, early, late, inject, weigh, back, reach, held, states, theirs,
     own_sem, part_send, part_recv, sums_send, sums_recv,
-    early_send, early_recv, late_send, late_recv, w_send, w_recv,
+    early_send, early_recv, late_send, late_recv, w_send, w_recv, word,
 ):
     ys, ks, rows, width, chunks = dims
     cw = width // chunks
@@ -34,12 +34,25 @@
     def other(i):
         return lax.rem(y + i, ys)
 
+    def greet(semaphore):
+        flip = d + 1 - 2 * lax.rem(d, 2)
+        pl.semaphore_signal(semaphore, inc=1, device_id=(me, flip), device_id_type=MESH)
+        for step in (2, -2):
+            near = d + step
+
+            @pl.when((near >= 0) & (near < ks))
+            def _():
+                pl.semaphore_signal(semaphore, inc=1, device_id=(me, near), device_id_type=MESH)
+
+    def greeted(semaphore, more):
+        inner = (d >= 2).astype(jnp.int32) + (d < ks - 2).astype(jnp.int32)
+        pl.semaphore_wait(semaphore, inner + 1 + more)
+
     barrier = pltpu.get_barrier_semaphore()
     pl.semaphore_signal(barrier, inc=1, device_id=(mate, d), device_id_type=MESH)
     for i in range(1, ys):
         pl.semaphore_signal(barrier, inc=1, device_id=(other(i) * 2 + c, d), device_id_type=MESH)
-    for i in range(1, ks):
-        pl.semaphore_signal(barrier, inc=1, device_id=(me, peer(i)), device_id_type=MESH)
+    greet(barrier)
 
     def slab(src, target, core, ch):
         at = pl.multiple_of((target * 2 + core) * width + ch * cw, LANES)
@@ -93,24 +106,32 @@
         )
 
     w_copy = pltpu.make_async_remote_copy(
-        src_ref=weights.at[0],
-        dst_ref=weights.at[1],
+        src_ref=weight,
+        dst_ref=theirs,
         send_sem=w_send,
         recv_sem=w_recv,
         device_id=(mate, d),
         device_id_type=MESH,
     )
 
-    for i, ch in order:
+    first_part, second_part = order[: (ys - 1) * chunks], order[(ys - 1) * chunks :]
+    for i, ch in first_part:
         for a in range(2):
             own_copy(i, ch, a).start()
-    weights[0] = 1.0 / jnp.full((SUB, LANES), count[0], jnp.int32).astype(jnp.float32)
-
-    pl.semaphore_wait(barrier, ys + ks - 1)
+
+    greeted(barrier, ys)
     w_copy.start()
-    for i, ch in order:
+    for i, ch in first_part:
         for a in range(2):
             part_copy(i, ch, a).start()
+
+    rounds = ks // 2 - 1
+    greet(word.at[0])
+
+    def pass_on(r):
+        greeted(word.at[r], 0)
+        if r + 1 < rounds:
+            greet(word.at[r + 1])
 
     sub = lax.broadcasted_iota(jnp.int32, (SUB, LANES), 0)
 
@@ -130,12 +151,26 @@
     def last(v):
         return jnp.broadcast_to(v[SUB - 1 : SUB], (SUB, LANES))
 
+    entries = table.shape[1]
+
+    def upright(row):
+        n = row.shape[1]
+        diagonal = lax.broadcasted_iota(jnp.int32, (n, n), 0) == lax.broadcasted_iota(
+            jnp.int32, (n, n), 1
+        )
+        return jnp.sum(
+            jnp.where(diagonal, jnp.broadcast_to(row, (n, n)), 0.0), axis=1, keepdims=True
+        )
+
+    level = lax.broadcasted_iota(jnp.int32, (entries, rows), 0)
+    hit = jnp.broadcast_to(index[...], (entries, rows)) == level
+    spread = jnp.broadcast_to(upright(table[...]), (entries, rows))
+    picked = upright(jnp.sum(jnp.where(hit, spread, 0.0), axis=0, keepdims=True))
+
     coef, through, before = [], [], []
     total = jnp.zeros((SUB, LANES), jnp.float32)
     for t in range(tiles):
-        v = jnp.zeros((SUB, LANES), jnp.float32)
-        for r in range(SUB):
-            v = jnp.where(sub == r, table[index[t * SUB + r]], v)
+        v = jnp.broadcast_to(picked[t * SUB : (t + 1) * SUB], (SUB, LANES))
         run = prefix(v) + total
         coef.append(v)
         through.append(run)
@@ -164,7 +199,7 @@
 
     def reduced(i, ch, a, zs, at):
         if a == 0:
-            w, v = weights[0], weights[1]
+            w, v = weight[...], theirs[...]
             return own[i, ch, 0, zs, at] * w + part[i, ch, 0, zs, at] * v
         return own[i, ch, 1, zs, at] + part[i, ch, 1, zs, at]
 
@@ -174,7 +209,7 @@
             part_copy(i, ch, a).wait_recv()
 
     w_copy.wait_recv()
-    for n, (i, ch) in enumerate(order[: (ys - 1) * chunks]):
+    for n, (i, ch) in enumerate(first_part):
         arrived(i, ch)
         for j in range(cols):
             at = pl.ds(j * LANES, LANES)
@@ -183,8 +218,18 @@
                 for a in range(2):
                     sums[i - 1, ch, a, zs, at] = reduced(i, ch, a, zs, at)
         sums_copy(i, ch).start()
-
+        if n == 0:
+            pass_on(0)
+
+    for i, ch in second_part:
+        for a in range(2):
+            own_copy(i, ch, a).start()
+            part_copy(i, ch, a).start()
+    if rounds > 1:
+        pass_on(1)
     terms()
+    for r in range(2, rounds):
+        pass_on(r)
     for i in range(1, ks):
         early_copy(i).start()
 
@@ -264,7 +309,7 @@
 def shards(ys, ks, grad_part, illum_part, source_count, rate, coef_table, coef_index):
     _, rows, lateral = grad_part.shape
     width = lateral // (2 * ys)
-    chunks = min(4, width // LANES)
+    chunks = min(2, width // LANES)
     cw = width // chunks
     cols = cw // LANES
     f32 = jnp.float32
@@ -273,12 +318,11 @@
     peers = (ys - 1, chunks, 2, rows, cw)
     field = pltpu.VMEM((rows, width), f32)
     anywhere = pl.BlockSpec(memory_space=pl.ANY)
-    scalars = pl.BlockSpec(memory_space=pltpu.SMEM)
     vmem = pl.BlockSpec(memory_space=pltpu.VMEM)
     return pl.pallas_call(
         functools.partial(body, (ys, ks, rows, width, chunks)),
         out_shape=jax.ShapeDtypeStruct((rows, width), f32),
-        in_specs=[anywhere, anywhere, scalars, vmem, scalars, scalars],
+        in_specs=[anywhere, anywhere, vmem, vmem, vmem, vmem],
         out_specs=vmem,
         scratch_shapes=[
             pltpu.VMEM(blocks, f32),
@@ -289,7 +333,7 @@
             pltpu.VMEM((ks, chunks, 2, cols, LANES), f32),
             field, field, field, field, field,
             pltpu.VMEM((2, width // LANES, LANES), f32),
-            pltpu.VMEM((2, SUB, LANES), f32),
+            pltpu.VMEM((SUB, LANES), f32),
             dma((ys, chunks, 2)),
             dma((ys, chunks, 2)),
             dma((ys, chunks, 2)),
@@ -301,9 +345,17 @@
             dma((ks - 1, chunks)),
             dma,
             dma,
+            pltpu.SemaphoreType.REGULAR((ks // 2 - 1,)),
         ],
-        compiler_params=pltpu.CompilerParams(collective_id=0, has_side_effects=True),
-    )(grad_part, illum_part, source_count, rate.reshape(1, -1), coef_table, coef_index)
+        compiler_params=pltpu.CompilerParams(collective_id=0, has_side_effects=True, vmem_limit_bytes=53 * 2**20),
+    )(
+        grad_part,
+        illum_part,
+        jnp.broadcast_to(1.0 / source_count.astype(f32)[:, None], (SUB, LANES)),
+        rate.reshape(1, -1),
+        coef_table.reshape(1, -1),
+        coef_index.reshape(1, -1),
+    )
 
 
 def solution(mesh):

time: 28.8 us -> 26.8 us (0.931)
  Pallas kernels: 26.2 us -> 24.5 us
  local copies, waits for them, and re-layouts: 1.67 us -> 1.36 us
    pallas_call x1, Pallas kernels: 26.2 us -> 24.5 us  [shards(): pl.pallas_call(functools.partial(body, (ys, ks, rows, width, chunks)), ou...]
    unnamed x1 -> x7, local copies, waits for them, and re-layouts: 1.67 us -> 1.35 us
where the time goes in v2:
time: 26.8 us; the launch traced here: 26.6 us
  Pallas kernels  24.5 us (91%)
  local copies, waits for them, and re-layouts  1.36 us (5%)
  between operations  0.73 us (3%)
    pallas_call x1, Pallas kernels, shards(): pl.pallas_call(functools.partial(body, (ys, ks, rows, width, chunks)), ou...  24.5 us
    unnamed x7, local copies, waits for them, and re-layouts  1.35 us

profile of v2, /device:TPU:0, one launch (start us, length us, event | category | flops | bytes accessed | tf_op | source)
XLA Modules:
  0.0 26.6 jit_solution(6960020483534144778)
XLA Ops:
  0.7 0.0 copy-start
  0.7 0.0 copy-start.1
  0.7 0.0 copy-start.2
  0.7 0.6 %copy-done = f32[2048]{0:T(1024)S(1)} copy-done((f32[2048]{0:T(1024)S(1)}, f32[2048]{0:T(1024)}, u32[]{:S(2)}) %copy-start) | copy-done | bytes 8216
  1.4 0.0 copy-done.1
  1.4 0.0 copy-done.2
  1.4 24.5 %shard_map.64 = f32[32,2048]{1,0:T(8,128)S(1)} custom-call(f32[1,32,8192]{2,1,0:T(8,128)} %grad.1, f32[1,32,8192]{2,1,0:T(8,128)} %illum.1, f32[8,128]{1,0:T(8,128)S(1)} %broadcast_in_dim.9.weight, f32[1,2048]{1,0:T(1,128)S(1)} %bitcast.4, f32[1,64]{1,0:T(1,128)S(1)} %bitcast.5, s32[1,32]{1,0:T(1,128)S(1)} %bitcast.6), custom_call_target="tpu_custom_call" | custom-call | tf_op jit(solution)/shard_map/pallas_call | solution.py:322
  25.9 0.7 %copy.9 = f32[32,2048]{1,0:T(8,128)} copy(f32[32,2048]{1,0:T(8,128)S(1)} %shard_map.64) | data formatting | bytes 524288
  (1 shorter events, 0.0 us)
Async XLA Ops:
  0.7 0.7 %copy-start = (f32[2048]{0:T(1024)S(1)}, f32[2048]{0:T(1024)}, u32[]{:S(2)}) copy-start(f32[2048]{0:T(1024)} %param.9) | copy-start | bytes 24580
  0.7 0.7 %copy-start.1 = (f32[64]{0:T(128)S(1)}, f32[64]{0:T(128)}, u32[]{:S(2)}) copy-start(f32[64]{0:T(128)} %param.10) | copy-start | bytes 772
  0.7 0.7 %copy-start.2 = (s32[32]{0:T(128)S(1)}, s32[32]{0:T(128)}, u32[]{:S(2)}) copy-start(s32[32]{0:T(128)} %param.11) | copy-start | bytes 388

commit v3 on v2

--- a/solution.py
+++ b/solution.py
@@ -19,9 +19,9 @@
     own_sem, part_send, part_recv, sums_send, sums_recv,
     early_send, early_recv, late_send, late_recv, w_send, w_recv, word,
 ):
-    ys, ks, rows, width, chunks = dims
-    cw = width // chunks
-    cols = cw // LANES
+    ys, ks, rows, width, counts = dims
+    chunks = len(counts)
+    starts = [sum(counts[:ch]) for ch in range(chunks)]
     tiles = rows // SUB
     me = lax.axis_index("shot")
     d = lax.axis_index("depth")
@@ -55,20 +55,23 @@
     greet(barrier)
 
     def slab(src, target, core, ch):
-        at = pl.multiple_of((target * 2 + core) * width + ch * cw, LANES)
-        return src.at[0, :, pl.ds(at, cw)]
+        at = pl.multiple_of((target * 2 + core) * width + starts[ch] * LANES, LANES)
+        return src.at[0, :, pl.ds(at, counts[ch] * LANES)]
+
+    def span(ch):
+        return pl.ds(0, counts[ch] * LANES)
 
     order = [(i, ch) for i in [*range(1, ys), 0] for ch in range(chunks)]
 
     def own_copy(i, ch, a):
         return pltpu.make_async_copy(
-            slab((grad, illum)[a], other(i), c, ch), own.at[i, ch, a], own_sem.at[i, ch, a]
+            slab((grad, illum)[a], other(i), c, ch), own.at[i, ch, a, :, span(ch)], own_sem.at[i, ch, a]
         )
 
     def part_copy(i, ch, a):
         return pltpu.make_async_remote_copy(
             src_ref=slab((grad, illum)[a], other(i), 1 - c, ch),
-            dst_ref=part.at[i, ch, a],
+            dst_ref=part.at[i, ch, a, :, span(ch)],
             send_sem=part_send.at[i, ch, a],
             recv_sem=part_recv.at[i, ch, a],
             device_id=(mate, d),
@@ -77,8 +80,8 @@
 
     def sums_copy(i, ch):
         return pltpu.make_async_remote_copy(
-            src_ref=sums.at[i - 1, ch],
-            dst_ref=landed.at[i - 1, ch],
+            src_ref=sums.at[i - 1, ch, :, :, span(ch)],
+            dst_ref=landed.at[i - 1, ch, :, :, span(ch)],
             send_sem=sums_send.at[i - 1, ch],
             recv_sem=sums_recv.at[i - 1, ch],
             device_id=(other(i) * 2 + c, d),
@@ -180,7 +183,6 @@
     def terms():
         for j in range(width // LANES):
             at = pl.ds(j * LANES, LANES)
-            ch, jj = j // cols, j % cols
             r = jnp.broadcast_to(rate[0:1, at], (SUB, LANES))
             tail = jnp.zeros((SUB, LANES), jnp.float32)
             for t in reversed(range(tiles)):
@@ -211,7 +213,7 @@
     w_copy.wait_recv()
     for n, (i, ch) in enumerate(first_part):
         arrived(i, ch)
-        for j in range(cols):
+        for j in range(counts[ch]):
             at = pl.ds(j * LANES, LANES)
             for t in range(tiles):
                 zs = pl.ds(t * SUB, SUB)
@@ -237,9 +239,9 @@
         arrived(0, ch)
         for i in range(1, ys):
             sums_copy(i, ch).wait_recv()
-        for j in range(cols):
+        for j in range(counts[ch]):
             at = pl.ds(j * LANES, LANES)
-            full = pl.ds(ch * cw + j * LANES, LANES)
+            full = pl.ds((starts[ch] + j) * LANES, LANES)
             carry = jnp.zeros((SUB, LANES), jnp.float32)
             parts = []
             for t in range(tiles):
@@ -251,7 +253,7 @@
                 run = prefix(inject[zs, full] * (num / den)) + carry
                 parts.append(run)
                 carry = last(run)
-            row = pl.ds(ch * cols + j, 1)
+            row = pl.ds(starts[ch] + j, 1)
             late[0, ch, 0, pl.ds(j, 1), :] = carry[0:1] * early[0, 0, row, :]
             tail = jnp.zeros((SUB, LANES), jnp.float32)
             for t in reversed(range(tiles)):
@@ -269,25 +271,26 @@
     for ch in range(chunks):
         for i in range(1, ks):
             late_copy(i, ch).wait_recv()
-        rs = pl.ds(ch * cols, cols)
+        cols = counts[ch]
+        rs = pl.ds(starts[ch], cols)
         state = jnp.zeros((cols, LANES), jnp.float32)
         mine = state
         ups = []
         for k in range(ks):
             slot = lax.rem(k - d + ks, ks)
             mine = jnp.where(k == d, state, mine)
-            ups.append(late[slot, ch, 1] + early[slot, 1, rs] * state)
+            ups.append(late[slot, ch, 1, :cols] + early[slot, 1, rs] * state)
             if k < ks - 1:
-                state = late[slot, ch, 0] + early[slot, 0, rs] * state
+                state = late[slot, ch, 0, :cols] + early[slot, 0, rs] * state
         up = jnp.zeros((cols, LANES), jnp.float32)
         for k in reversed(range(1, ks)):
             slot = lax.rem(k - d + ks, ks)
             up = jnp.where(k > d, ups[k] + early[slot, 0, rs] * up, up)
         states[0, rs] = mine
         states[1, rs] = up * early[0, 0, rs]
-        for j in range(cols):
-            row = pl.ds(ch * cols + j, 1)
-            full = pl.ds(ch * cw + j * LANES, LANES)
+        for j in range(counts[ch]):
+            row = pl.ds(starts[ch] + j, 1)
+            full = pl.ds((starts[ch] + j) * LANES, LANES)
             e = jnp.broadcast_to(states[0, row, :], (SUB, LANES))
             b = jnp.broadcast_to(states[1, row, :], (SUB, LANES))
             for t in range(tiles):
@@ -309,9 +312,12 @@
 def shards(ys, ks, grad_part, illum_part, source_count, rate, coef_table, coef_index):
     _, rows, lateral = grad_part.shape
     width = lateral // (2 * ys)
-    chunks = min(2, width // LANES)
-    cw = width // chunks
-    cols = cw // LANES
+    blocks_across = width // LANES
+    lead = max(1, blocks_across // 8)
+    half = blocks_across // 2
+    counts = (lead, half, blocks_across - lead - half)
+    chunks, cols = len(counts), half
+    cw = cols * LANES
     f32 = jnp.float32
     dma = pltpu.SemaphoreType.DMA
     blocks = (ys, chunks, 2, rows, cw)
@@ -320,7 +326,7 @@
     anywhere = pl.BlockSpec(memory_space=pl.ANY)
     vmem = pl.BlockSpec(memory_space=pltpu.VMEM)
     return pl.pallas_call(
-        functools.partial(body, (ys, ks, rows, width, chunks)),
+        functools.partial(body, (ys, ks, rows, width, counts)),
         out_shape=jax.ShapeDtypeStruct((rows, width), f32),
         in_specs=[anywhere, anywhere, vmem, vmem, vmem, vmem],
         out_specs=vmem,

time: 26.8 us -> 26.7 us (level)
  no operation moved by 1% of the time
where the time goes in v3:
time: 26.7 us; the launch traced here: 26.5 us
  Pallas kernels  24.4 us (91%)
  local copies, waits for them, and re-layouts  1.36 us (5%)
  between operations  0.73 us (3%)
    pallas_call x1, Pallas kernels, shards(): pl.pallas_call(functools.partial(body, (ys, ks, rows, width, counts)), ou...  24.4 us
    unnamed x7, local copies, waits for them, and re-layouts  1.35 us

profile of v3, /device:TPU:0, one launch (start us, length us, event | category | flops | bytes accessed | tf_op | source)
XLA Modules:
  0.0 26.5 jit_solution(3098155463062293381)
XLA Ops:
  0.7 0.0 copy-start
  0.7 0.0 copy-start.1
  0.7 0.0 copy-start.2
  0.7 0.6 %copy-done = f32[2048]{0:T(1024)S(1)} copy-done((f32[2048]{0:T(1024)S(1)}, f32[2048]{0:T(1024)}, u32[]{:S(2)}) %copy-start) | copy-done | bytes 8216
  1.4 0.0 copy-done.1
  1.4 0.0 copy-done.2
  1.4 24.4 %shard_map.64 = f32[32,2048]{1,0:T(8,128)S(1)} custom-call(f32[1,32,8192]{2,1,0:T(8,128)} %grad.1, f32[1,32,8192]{2,1,0:T(8,128)} %illum.1, f32[8,128]{1,0:T(8,128)S(1)} %broadcast_in_dim.9.weight, f32[1,2048]{1,0:T(1,128)S(1)} %bitcast.4, f32[1,64]{1,0:T(1,128)S(1)} %bitcast.5, s32[1,32]{1,0:T(1,128)S(1)} %bitcast.6), custom_call_target="tpu_custom_call" | custom-call | tf_op jit(solution)/shard_map/pallas_call | solution.py:328
  25.8 0.7 %copy.9 = f32[32,2048]{1,0:T(8,128)} copy(f32[32,2048]{1,0:T(8,128)S(1)} %shard_map.64) | data formatting | bytes 524288
  (1 shorter events, 0.0 us)
Async XLA Ops:
  0.7 0.7 %copy-start = (f32[2048]{0:T(1024)S(1)}, f32[2048]{0:T(1024)}, u32[]{:S(2)}) copy-start(f32[2048]{0:T(1024)} %param.9) | copy-start | bytes 24580
  0.7 0.7 %copy-start.1 = (f32[64]{0:T(128)S(1)}, f32[64]{0:T(128)}, u32[]{:S(2)}) copy-start(f32[64]{0:T(128)} %param.10) | copy-start | bytes 772
  0.7 0.7 %copy-start.2 = (s32[32]{0:T(128)S(1)}, s32[32]{0:T(128)}, u32[]{:S(2)}) copy-start(s32[32]{0:T(128)} %param.11) | copy-start | bytes 388
